TPU v7x, 128 devices: a whole 4x4x4 slice. The times are simulated.
128 devices in a mesh: strike: 8 (over z, x_hi), normal: 16 (over x_lo, y, core).
Axes of the slice: x: 4 (x_hi: 2, x_lo: 2; x = x_hi * 2 + x_lo), y: 4, z: 4, core: 2. Of those that a mesh axis runs over, the one named last changes fastest.
Arguments:
- velocity: float32 [3, 256, 256, 384], P(None, 'strike', 'normal'), may hold values from -6 to 6
- stress: float32 [6, 256, 256, 384], P(None, 'strike', 'normal'), may hold values from -6 to 6
- modulus: float32 [256, 256, 384], P('strike', 'normal'), may hold values from 0.5 to 2
- buoyancy: float32 [256, 256, 384], P('strike', 'normal'), may hold values from 0.5 to 1.5
- fault_state: float32 [256, 384], P(('strike', 'normal')), may hold values from -0.3 to 0.3
- fault_mask: int32 [256, 384], P(('strike', 'normal')), may hold values 0 or 1
- region_ids: int32 [256, 384], P(('strike', 'normal')), may hold values from 0 to 3
- friction_table: float32 [4, 4], replicated, may hold values from 0.2 to 2
Outputs:
- velocity_out: float32 [3, 256, 256, 384], P(None, 'strike', 'normal')
- stress_out: float32 [6, 256, 256, 384], P(None, 'strike', 'normal')
- slip_rate: float32 [256, 384], P(('strike', 'normal'))
- state_out: float32 [256, 384], P(('strike', 'normal'))
Inputs may be any that keep to these rules, and one draw needn't show every extreme that they name: `region_ids`: region ids index the columns of friction_table.
All inputs are finite; a program needn't handle non-finite values. No bound on the sum of `fault_mask` on one device may be relied on, other than what follows from the above.
Results may differ from a plain program's by a relative error of at most 0.0003.
Values sent between devices are 32-bit elements; how exact they have to be, the bound alone decides.
No kernel may reach another device: no remote copies, remote signals or barrier semaphores. Data moves between devices by JAX's collectives and lax.ppermute only.
A program may use at most 128 MiB of HBM per device.

v0:
```python
import jax
import jax.numpy as jnp
from jax import lax
from jax.sharding import PartitionSpec as P

STEPS = 2
NEWTON = 4
inner_coef = 9.0 / 8.0
outer_coef = -1.0 / 24.0
time_step = 0.1
impedance = 1.0


def with_halo(cells, sides, width):
    for axis, dim in sides:
        count = lax.axis_size(axis)
        ends = count - 1
        head = lax.slice_in_dim(cells, 0, width, axis=dim)
        tail = lax.slice_in_dim(cells, cells.shape[dim] - width, cells.shape[dim], axis=dim)
        cells = jnp.concatenate(
            [
                lax.ppermute(tail, axis, [(i, (i + 1) % count) for i in range(ends)]),
                cells,
                lax.ppermute(head, axis, [((i + 1) % count, i) for i in range(ends)]),
            ],
            axis=dim,
        )
    return cells


def inverse_sinh(values):
    magnitude = jnp.abs(values)
    root = jnp.sqrt(1.0 + magnitude * magnitude)
    result = jnp.log1p(magnitude + magnitude * magnitude / (1.0 + root))
    return jnp.where(values < 0.0, -result, result)


def shifted(padded_values, dimension, offset):
    length = padded_values.shape[dimension] - 4
    return lax.slice_in_dim(padded_values, 2 + offset, 2 + offset + length, axis=dimension)


def forward_diff(padded_values, dimension):
    return inner_coef * (
        shifted(padded_values, dimension, 1) - shifted(padded_values, dimension, 0)
    ) + outer_coef * (shifted(padded_values, dimension, 2) - shifted(padded_values, dimension, -1))


def backward_diff(padded_values, dimension):
    return inner_coef * (
        shifted(padded_values, dimension, 0) - shifted(padded_values, dimension, -1)
    ) + outer_coef * (shifted(padded_values, dimension, 1) - shifted(padded_values, dimension, -2))


def padded(values, dimension):
    widths = [(0, 0)] * values.ndim
    widths[dimension] = (2, 2)
    return jnp.pad(values, widths)


def accelerate(sxx_x, sxy_x, sxz_x, syy_y, sxy_y, syz_y, sxz, syz, szz):
    accel_x = forward_diff(sxx_x, 0) + backward_diff(sxy_y, 1) + backward_diff(padded(sxz, 2), 2)
    accel_y = backward_diff(sxy_x, 0) + forward_diff(syy_y, 1) + backward_diff(padded(syz, 2), 2)
    accel_z = backward_diff(sxz_x, 0) + backward_diff(syz_y, 1) + forward_diff(padded(szz, 2), 2)
    return jnp.stack((accel_x, accel_y, accel_z))


def strain_rates(vx_x, vy_x, vz_x, vx_y, vy_y, vz_y, vel_x, vel_y, vel_z):
    exx = backward_diff(vx_x, 0)
    eyy = backward_diff(vy_y, 1)
    ezz = backward_diff(padded(vel_z, 2), 2)
    trace = exx + eyy + ezz
    rate_xy = forward_diff(vx_y, 1) + forward_diff(vy_x, 0)
    rate_xz = forward_diff(padded(vel_x, 2), 2) + forward_diff(vz_x, 0)
    rate_yz = forward_diff(padded(vel_y, 2), 2) + forward_diff(vz_y, 1)
    return jnp.stack(
        (trace + 2.0 * exx, trace + 2.0 * eyy, trace + 2.0 * ezz, rate_xy, rate_xz, rate_yz)
    )


def lookup(regions, friction_table):
    labels = jnp.arange(friction_table.shape[1], dtype=jnp.float32)
    onehot = (regions[None] == labels[:, None, None]).astype(jnp.float32)
    return jnp.einsum("cr,rxz->cxz", friction_table, onehot, precision=lax.Precision.HIGHEST)


def friction(minus, plus, traction, state_now, mask_now, params):
    direct_effect = params[0]
    evolution_b = params[1]
    inverse_length = params[2]
    normal_stress = params[3]
    locked = traction + impedance * (plus - minus)
    scale_c = 0.5 * jnp.exp(state_now / direct_effect)
    weight = normal_stress * direct_effect
    rate = jnp.zeros_like(locked)
    for newton_step in range(NEWTON):
        argument = scale_c * rate
        residue = locked - impedance * rate - weight * inverse_sinh(argument)
        slope = impedance + weight * scale_c / jnp.sqrt(1.0 + argument * argument)
        rate = rate + residue / slope
    rate = rate * mask_now
    traction_new = locked - impedance * rate
    middle = 0.5 * (minus + plus)
    state_new = state_now + time_step * inverse_length * (
        jnp.exp(-state_now / evolution_b) - jnp.abs(rate)
    )
    return (rate, traction_new, middle - 0.5 * rate, middle + 0.5 * rate, state_new)


def local(velocity, stress, modulus, buoyancy, fault_state, fault_mask, region_ids, friction_table):
    members = lax.axis_size("normal")
    position = lax.axis_index("normal")
    minus_device = position == members // 2 - 1
    plus_device = position == members // 2
    owned_rows = fault_state.shape[0]
    last_row = velocity.shape[2] - 1
    state_now = fault_state
    mask_now = fault_mask.astype(jnp.float32)
    regions = region_ids.astype(jnp.float32)
    params = lookup(regions, friction_table)
    rate = jnp.zeros_like(state_now)
    for time_index in range(STEPS):
        whole_rims = with_halo(stress, (("strike", 1), ("normal", 2)), 2)
        along_x = whole_rims[:, :, 2:-2]
        along_y = whole_rims[:, 2:-2]
        sxx_x, sxy_x, sxz_x = (along_x[0], along_x[3], along_x[4])
        syy_y, sxy_y, syz_y = (along_y[1], along_y[3], along_y[5])
        accel = accelerate(
            sxx_x, sxy_x, sxz_x, syy_y, sxy_y, syz_y, stress[4], stress[5], stress[2]
        )
        velocity = velocity + time_step * buoyancy * accel
        vel_x = velocity[0]
        minus_row = vel_x[:, last_row, :]
        plus_here = vel_x[:, 0, :]
        traction_row = stress[3][:, last_row, :]
        blank = jnp.zeros_like(minus_row)
        contrib = jnp.stack(
            (
                jnp.where(minus_device, minus_row, blank),
                jnp.where(plus_device, plus_here, blank),
                jnp.where(minus_device, traction_row, blank),
            )
        )
        rows_all = lax.psum(contrib, "normal")
        mine = lax.dynamic_slice_in_dim(rows_all, position * owned_rows, owned_rows, 1)
        rate, traction_own, minus_own, plus_own, state_now = friction(
            mine[0], mine[1], mine[2], state_now, mask_now, params
        )
        returned = lax.all_gather(
            jnp.stack((minus_own, plus_own, traction_own)), "normal", axis=1, tiled=True
        )
        minus_full, plus_full, traction_full = (returned[0], returned[1], returned[2])
        new_last = jnp.where(minus_device, minus_full, minus_row)
        new_first = jnp.where(plus_device, plus_full, plus_here)
        vel_x = vel_x.at[:, last_row, :].set(new_last).at[:, 0, :].set(new_first)
        velocity = velocity.at[0].set(vel_x)
        vel_rims = with_halo(velocity, (("strike", 1), ("normal", 2)), 2)
        vel_along_x = vel_rims[:, :, 2:-2]
        vel_along_y = vel_rims[:, 2:-2]
        rates = strain_rates(
            vel_along_x[0],
            vel_along_x[1],
            vel_along_x[2],
            vel_along_y[0],
            vel_along_y[1],
            vel_along_y[2],
            velocity[0],
            velocity[1],
            velocity[2],
        )
        stress = stress + time_step * modulus * rates
        fault_layer = jnp.where(minus_device, traction_full, stress[3][:, last_row, :])
        stress = stress.at[3, :, last_row, :].set(fault_layer)
    return (velocity, stress, rate, state_now)


def solution(mesh):
    return jax.shard_map(
        local,
        mesh=mesh,
        in_specs=(
            P(None, "strike", "normal", None),
            P(None, "strike", "normal", None),
            P("strike", "normal", None),
            P("strike", "normal", None),
            P(("strike", "normal"), None),
            P(("strike", "normal"), None),
            P(("strike", "normal"), None),
            P(),
        ),
        out_specs=(
            P(None, "strike", "normal", None),
            P(None, "strike", "normal", None),
            P(("strike", "normal"), None),
            P(("strike", "normal"), None),
        ),
        check_vma=False,
    )
```

profile of v0, /device:TPU:29, one launch (start us, length us, event | category | flops | bytes accessed | tf_op | source)
XLA Modules:
  0.0 442.2 jit_solution(4840027687795716641)
XLA Ops:
  7.2 6.1 %constant_dynamic-update-slice_fusion.1 = (f32[6,34,16,384]{3,1,2,0:T(8,128)}, f32[6,32,16,384]{3,1,2,0:T(8,128)S(1)}) fusion(f32[6,32,16,384]{3,2,1,0:T(8,128)} %param.25), kind=kLoop, calls=%fused_computation.427 | loop fusion | bytes 14155776
  16.5 3.5 collective-permute-start.1
  23.8 4.1 collective-permute-done.1
  27.9 7.7 %collective-permute-done = f32[6,2,16,384]{3,1,2,0:T(2,128)S(1)} collective-permute-done((f32[6,2,16,384]{3,1,2,0:T(2,128)S(1)}, f32[6,2,16,384]{3,1,2,0:T(2,128)S(1)}, u32[]{:S(2)}, u32[]{:S(2)}) %collective-permute-start) | collective-permute-done | bytes 294944 | tf_op jit(solution)/shard_map/ppermute | solution.py:24
  37.6 4.0 collective-permute-start.2
  44.4 4.8 %collective-permute-done.2 = f32[6,36,2,384]{3,2,1,0:T(2,128)S(1)} collective-permute-done((f32[6,36,2,384]{3,2,1,0:T(2,128)S(1)}, f32[6,36,2,384]{3,2,1,0:T(2,128)S(1)}, u32[]{:S(2)}, u32[]{:S(2)}) %collective-permute-start.2) | collective-permute-done | bytes 663584 | tf_op jit(solution)/shard_map/ppermute | solution.py:22
  49.3 6.8 %collective-permute-done.3 = f32[6,36,2,384]{3,2,1,0:T(2,128)S(1)} collective-permute-done((f32[6,36,2,384]{3,2,1,0:T(2,128)S(1)}, f32[6,36,2,384]{3,2,1,0:T(2,128)S(1)}, u32[]{:S(2)}, u32[]{:S(2)}) %collective-permute-start.3) | collective-permute-done | bytes 663584 | tf_op jit(solution)/shard_map/ppermute | solution.py:24
  62.5 108.5 %all-reduce.15.cloned.1.call-done = f32[3,32,384]{2,1,0:T(8,128)} async-done(((f32[3,32,384]{2,1,0:T(8,128)}), f32[3,32,384]{2,1,0:T(8,128)}) %all-reduce.15.cloned.1.call-update) | async-done | bytes 147472 | tf_op jit(solution)/shard_map/psum | solution.py:144
  172.7 14.7 %all_gather.6 = f32[3,32,384]{2,0,1:T(4,128)S(1)} all-gather(f32[3,2,384]{2,0,1:T(4,128)S(1)} %copy.49), channel_id=1, replica_groups=mesh['strike'=8,'normal'=16] {'normal'}, dimensions={1}, use_global_device_ids=true | all-gather | bytes 156672 | tf_op jit(solution)/shard_map/all_gather | solution.py:149
  192.5 3.6 collective-permute-start.5
  198.0 3.9 collective-permute-done.5
  202.0 6.8 %collective-permute-start.6 = (f32[3,36,2,384]{3,1,2,0:T(8,128)S(1)}, f32[3,36,2,384]{3,1,2,0:T(8,128)S(1)}, u32[]{:S(2)}, u32[]{:S(2)}) collective-permute-start(f32[3,36,2,384]{3,1,2,0:T(8,128)S(1)} %get-tuple-element.154), channel_id=1, source_target_pairs={{0,1},{1,2},{2,3},{3,4},{4,5},{5,6},{6,7},{7,8},{8,9},{9,10},{10,1... | collective-permute-start | bytes 995336 | tf_op jit(solution)/shard_map/ppermute | solution.py:22
  213.2 6.5 %collective-permute-done.7 = f32[3,36,2,384]{3,1,2,0:T(8,128)S(1)} collective-permute-done((f32[3,36,2,384]{3,1,2,0:T(8,128)S(1)}, f32[3,36,2,384]{3,1,2,0:T(8,128)S(1)}, u32[]{:S(2)}, u32[]{:S(2)}) %collective-permute-start.7) | collective-permute-done | bytes 331808 | tf_op jit(solution)/shard_map/ppermute | solution.py:24
  228.3 5.8 %collective-permute-start.9 = (f32[6,2,16,384]{3,1,2,0:T(2,128)S(1)}, f32[6,2,16,384]{3,1,2,0:T(2,128)S(1)}, u32[]{:S(2)}, u32[]{:S(2)}) collective-permute-start(f32[6,2,16,384]{3,1,2,0:T(2,128)S(1)} %get-tuple-element.136), channel_id=1, source_target_pairs={{0,16},{16,32},{32,48},{48,64},{64,80},{80,96},{96,112},{1,17},{17... | collective-permute-start | bytes 884744 | tf_op jit(solution)/shard_map/ppermute | solution.py:22
  238.8 4.1 collective-permute-start.10
  245.4 5.1 %collective-permute-done.10 = f32[6,36,2,384]{3,2,1,0:T(2,128)S(1)} collective-permute-done((f32[6,36,2,384]{3,2,1,0:T(2,128)S(1)}, f32[6,36,2,384]{3,2,1,0:T(2,128)S(1)}, u32[]{:S(2)}, u32[]{:S(2)}) %collective-permute-start.10) | collective-permute-done | bytes 663584 | tf_op jit(solution)/shard_map/ppermute | solution.py:22
  250.5 6.8 %collective-permute-done.11 = f32[6,36,2,384]{3,2,1,0:T(2,128)S(1)} collective-permute-done((f32[6,36,2,384]{3,2,1,0:T(2,128)S(1)}, f32[6,36,2,384]{3,2,1,0:T(2,128)S(1)}, u32[]{:S(2)}, u32[]{:S(2)}) %collective-permute-start.11) | collective-permute-done | bytes 663584 | tf_op jit(solution)/shard_map/ppermute | solution.py:24
  263.5 111.2 %all-reduce.17.cloned.1.call-done = f32[3,32,384]{2,1,0:T(8,128)} async-done(((f32[3,32,384]{2,1,0:T(8,128)}), f32[3,32,384]{2,1,0:T(8,128)}) %all-reduce.17.cloned.1.call-update) | async-done | bytes 147472 | tf_op jit(solution)/shard_map/psum | solution.py:144
  377.0 14.9 %all_gather.7 = f32[3,32,384]{2,0,1:T(4,128)S(1)} all-gather(f32[3,2,384]{2,0,1:T(4,128)S(1)} %copy.60), channel_id=1, replica_groups=mesh['strike'=8,'normal'=16] {'normal'}, dimensions={1}, use_global_device_ids=true | all-gather | bytes 156672 | tf_op jit(solution)/shard_map/all_gather | solution.py:149
  397.0 3.6 collective-permute-start.13
  402.5 3.9 collective-permute-done.13
  406.5 6.8 %collective-permute-start.14 = (f32[3,36,2,384]{3,1,2,0:T(8,128)S(1)}, f32[3,36,2,384]{3,1,2,0:T(8,128)S(1)}, u32[]{:S(2)}, u32[]{:S(2)}) collective-permute-start(f32[3,36,2,384]{3,1,2,0:T(8,128)S(1)} %get-tuple-element.152), channel_id=1, source_target_pairs={{0,1},{1,2},{2,3},{3,4},{4,5},{5,6},{6,7},{7,8},{8,9},{9,10},{10,1... | collective-permute-start | bytes 995336 | tf_op jit(solution)/shard_map/ppermute | solution.py:22
  418.0 6.2 %collective-permute-done.15 = f32[3,36,2,384]{3,1,2,0:T(8,128)S(1)} collective-permute-done((f32[3,36,2,384]{3,1,2,0:T(8,128)S(1)}, f32[3,36,2,384]{3,1,2,0:T(8,128)S(1)}, u32[]{:S(2)}, u32[]{:S(2)}) %collective-permute-start.15) | collective-permute-done | bytes 331808 | tf_op jit(solution)/shard_map/ppermute | solution.py:24
  430.5 4.9 %copy.65 = f32[6,32,16,384]{3,2,1,0:T(8,128)} copy(f32[6,32,16,384]{3,1,2,0:T(8,128)S(1)} %fusion.225) | data formatting | bytes 9437184
  (158 shorter events, 73.1 us)
Async XLA Ops:
  7.2 163.7 %all-reduce.15.cloned.1.call-start = ((), (), s32[]{:S(2)}) async-start(), calls=%async_computation | async-start | bytes 294912 | tf_op jit(solution)/shard_map/psum | solution.py:144
  16.5 11.5 %collective-permute-start.1 = (f32[6,2,16,384]{3,1,2,0:T(2,128)}, f32[6,2,16,384]{3,1,2,0:T(2,128)S(1)}, u32[]{:S(2)}, u32[]{:S(2)}) collective-permute-start(f32[6,2,16,384]{3,1,2,0:T(2,128)} %get-tuple-element.144), channel_id=1, source_target_pairs={{0,16},{16,32},{32,48},{48,64},{64,80},{80,96},{96,112},{1,17},{17... | collective-permute-start | bytes 884744 | tf_op jit(solution)/shard_map/ppermute | solution.py:22
  20.0 15.7 %collective-permute-start = (f32[6,2,16,384]{3,1,2,0:T(2,128)S(1)}, f32[6,2,16,384]{3,1,2,0:T(2,128)S(1)}, u32[]{:S(2)}, u32[]{:S(2)}) collective-permute-start(f32[6,2,16,384]{3,1,2,0:T(2,128)S(1)} %get-tuple-element.145), channel_id=1, source_target_pairs={{16,0},{32,16},{48,32},{64,48},{80,64},{96,80},{112,96},{17,1},{33... | collective-permute-start | bytes 884744 | tf_op jit(solution)/shard_map/ppermute | solution.py:24
  23.6 35.2 %copy-start.8 = (f32[32,16,384]{2,0,1:T(8,128)}, f32[32,16,384]{2,0,1:T(8,128)S(1)}, u32[]{:S(2)}) copy-start(f32[32,16,384]{2,0,1:T(8,128)S(1)} %copy.31) | copy-start | bytes 2359300
  37.6 11.7 %collective-permute-start.2 = (f32[6,36,2,384]{3,2,1,0:T(2,128)S(1)}, f32[6,36,2,384]{3,2,1,0:T(2,128)S(1)}, u32[]{:S(2)}, u32[]{:S(2)}) collective-permute-start(f32[6,36,2,384]{3,2,1,0:T(2,128)S(1)} %copy.38), channel_id=1, source_target_pairs={{0,1},{1,2},{2,3},{3,4},{4,5},{5,6},{6,7},{7,8},{8,9},{9,10},{10,1... | collective-permute-start | bytes 1990664 | tf_op jit(solution)/shard_map/ppermute | solution.py:22
  42.0 14.1 %collective-permute-start.3 = (f32[6,36,2,384]{3,2,1,0:T(2,128)S(1)}, f32[6,36,2,384]{3,2,1,0:T(2,128)S(1)}, u32[]{:S(2)}, u32[]{:S(2)}) collective-permute-start(f32[6,36,2,384]{3,2,1,0:T(2,128)S(1)} %copy.39), channel_id=1, source_target_pairs={{1,0},{2,1},{3,2},{4,3},{5,4},{6,5},{7,6},{8,7},{9,8},{10,9},{11,1... | collective-permute-start | bytes 1990664 | tf_op jit(solution)/shard_map/ppermute | solution.py:24
  59.7 111.2 %copy-start.15 = (s32[2,384]{1,0:T(2,128)S(1)}, s32[2,384]{1,0:T(2,128)}, u32[]{:S(2)}) copy-start(s32[2,384]{1,0:T(2,128)} %param.29) | copy-start | bytes 9220
  59.7 111.2 %copy-start.17 = (f32[2,384]{1,0:T(2,128)S(1)}, f32[2,384]{1,0:T(2,128)}, u32[]{:S(2)}) copy-start(f32[2,384]{1,0:T(2,128)} %param.28) | copy-start | bytes 9220
  62.4 312.3 %all-reduce.17.cloned.1.call-start = ((), (), s32[]{:S(2)}) async-start(), calls=%async_computation.1 | async-start | bytes 294912 | tf_op jit(solution)/shard_map/psum | solution.py:144
  170.9 39.9 %copy-start.14 = (f32[32,16,384]{2,1,0:T(8,128)S(1)}, f32[32,16,384]{2,1,0:T(8,128)}, u32[]{:S(2)}) copy-start(f32[32,16,384]{2,1,0:T(8,128)} %param.26) | copy-start | bytes 2359300
  189.3 8.7 %collective-permute-start.4 = (f32[3,2,16,384]{3,1,2,0:T(2,128)S(1)}, f32[3,2,16,384]{3,1,2,0:T(2,128)S(1)}, u32[]{:S(2)}, u32[]{:S(2)}) collective-permute-start(f32[3,2,16,384]{3,1,2,0:T(2,128)S(1)} %get-tuple-element.162), channel_id=1, source_target_pairs={{0,16},{16,32},{32,48},{48,64},{64,80},{80,96},{96,112},{1,17},{17... | collective-permute-start | bytes 442376 | tf_op jit(solution)/shard_map/ppermute | solution.py:22
  192.5 9.4 %collective-permute-start.5 = (f32[3,2,16,384]{3,1,2,0:T(2,128)S(1)}, f32[3,2,16,384]{3,1,2,0:T(2,128)S(1)}, u32[]{:S(2)}, u32[]{:S(2)}) collective-permute-start(f32[3,2,16,384]{3,1,2,0:T(2,128)S(1)} %get-tuple-element.163), channel_id=1, source_target_pairs={{16,0},{32,16},{48,32},{64,48},{80,64},{96,80},{112,96},{17,1},{33... | collective-permute-start | bytes 442376 | tf_op jit(solution)/shard_map/ppermute | solution.py:24
  202.0 11.2 %collective-permute-start.6 = (f32[3,36,2,384]{3,1,2,0:T(8,128)S(1)}, f32[3,36,2,384]{3,1,2,0:T(8,128)S(1)}, u32[]{:S(2)}, u32[]{:S(2)}) collective-permute-start(f32[3,36,2,384]{3,1,2,0:T(8,128)S(1)} %get-tuple-element.154), channel_id=1, source_target_pairs={{0,1},{1,2},{2,3},{3,4},{4,5},{5,6},{6,7},{7,8},{8,9},{9,10},{10,1... | collective-permute-start | bytes 995336 | tf_op jit(solution)/shard_map/ppermute | solution.py:22
  208.7 10.9 %collective-permute-start.7 = (f32[3,36,2,384]{3,1,2,0:T(8,128)S(1)}, f32[3,36,2,384]{3,1,2,0:T(8,128)S(1)}, u32[]{:S(2)}, u32[]{:S(2)}) collective-permute-start(f32[3,36,2,384]{3,1,2,0:T(8,128)S(1)} %get-tuple-element.155), channel_id=1, source_target_pairs={{1,0},{2,1},{3,2},{4,3},{5,4},{6,5},{7,6},{8,7},{9,8},{10,9},{11,1... | collective-permute-start | bytes 995336 | tf_op jit(solution)/shard_map/ppermute | solution.py:24
  226.1 33.3 %copy-start.2 = (f32[6,32,16,384]{3,1,2,0:T(8,128)}, f32[6,32,16,384]{3,1,2,0:T(8,128)S(1)}, u32[]{:S(2)}) copy-start(f32[6,32,16,384]{3,1,2,0:T(8,128)S(1)} %fusion.228) | copy-start | bytes 14155780
  226.3 10.7 %collective-permute-start.8 = (f32[6,2,16,384]{3,1,2,0:T(2,128)S(1)}, f32[6,2,16,384]{3,1,2,0:T(2,128)S(1)}, u32[]{:S(2)}, u32[]{:S(2)}) collective-permute-start(f32[6,2,16,384]{3,1,2,0:T(2,128)S(1)} %get-tuple-element.137), channel_id=1, source_target_pairs={{16,0},{32,16},{48,32},{64,48},{80,64},{96,80},{112,96},{17,1},{33... | collective-permute-start | bytes 884744 | tf_op jit(solution)/shard_map/ppermute | solution.py:24
  228.3 10.0 %collective-permute-start.9 = (f32[6,2,16,384]{3,1,2,0:T(2,128)S(1)}, f32[6,2,16,384]{3,1,2,0:T(2,128)S(1)}, u32[]{:S(2)}, u32[]{:S(2)}) collective-permute-start(f32[6,2,16,384]{3,1,2,0:T(2,128)S(1)} %get-tuple-element.136), channel_id=1, source_target_pairs={{0,16},{16,32},{32,48},{48,64},{64,80},{80,96},{96,112},{1,17},{17... | collective-permute-start | bytes 884744 | tf_op jit(solution)/shard_map/ppermute | solution.py:22
  238.8 11.7 %collective-permute-start.10 = (f32[6,36,2,384]{3,2,1,0:T(2,128)S(1)}, f32[6,36,2,384]{3,2,1,0:T(2,128)S(1)}, u32[]{:S(2)}, u32[]{:S(2)}) collective-permute-start(f32[6,36,2,384]{3,2,1,0:T(2,128)S(1)} %copy.55), channel_id=1, source_target_pairs={{0,1},{1,2},{2,3},{3,4},{4,5},{5,6},{6,7},{7,8},{8,9},{9,10},{10,1... | collective-permute-start | bytes 1990664 | tf_op jit(solution)/shard_map/ppermute | solution.py:22
  243.2 14.1 %collective-permute-start.11 = (f32[6,36,2,384]{3,2,1,0:T(2,128)S(1)}, f32[6,36,2,384]{3,2,1,0:T(2,128)S(1)}, u32[]{:S(2)}, u32[]{:S(2)}) collective-permute-start(f32[6,36,2,384]{3,2,1,0:T(2,128)S(1)} %copy.56), channel_id=1, source_target_pairs={{1,0},{2,1},{3,2},{4,3},{5,4},{6,5},{7,6},{8,7},{9,8},{10,9},{11,1... | collective-permute-start | bytes 1990664 | tf_op jit(solution)/shard_map/ppermute | solution.py:24
  376.2 41.7 %copy-start.16 = (f32[2,384]{1,0:T(2,128)}, f32[2,384]{1,0:T(2,128)S(1)}, u32[]{:S(2)}) copy-start(f32[2,384]{1,0:T(2,128)S(1)} %get-tuple-element.109) | copy-start | bytes 9220
  393.8 8.7 %collective-permute-start.12 = (f32[3,2,16,384]{3,1,2,0:T(2,128)S(1)}, f32[3,2,16,384]{3,1,2,0:T(2,128)S(1)}, u32[]{:S(2)}, u32[]{:S(2)}) collective-permute-start(f32[3,2,16,384]{3,1,2,0:T(2,128)S(1)} %get-tuple-element.157), channel_id=1, source_target_pairs={{0,16},{16,32},{32,48},{48,64},{64,80},{80,96},{96,112},{1,17},{17... | collective-permute-start | bytes 442376 | tf_op jit(solution)/shard_map/ppermute | solution.py:22
  397.0 9.4 %collective-permute-start.13 = (f32[3,2,16,384]{3,1,2,0:T(2,128)S(1)}, f32[3,2,16,384]{3,1,2,0:T(2,128)S(1)}, u32[]{:S(2)}, u32[]{:S(2)}) collective-permute-start(f32[3,2,16,384]{3,1,2,0:T(2,128)S(1)} %get-tuple-element.158), channel_id=1, source_target_pairs={{16,0},{32,16},{48,32},{64,48},{80,64},{96,80},{112,96},{17,1},{33... | collective-permute-start | bytes 442376 | tf_op jit(solution)/shard_map/ppermute | solution.py:24
  406.5 11.5 %collective-permute-start.14 = (f32[3,36,2,384]{3,1,2,0:T(8,128)S(1)}, f32[3,36,2,384]{3,1,2,0:T(8,128)S(1)}, u32[]{:S(2)}, u32[]{:S(2)}) collective-permute-start(f32[3,36,2,384]{3,1,2,0:T(8,128)S(1)} %get-tuple-element.152), channel_id=1, source_target_pairs={{0,1},{1,2},{2,3},{3,4},{4,5},{5,6},{6,7},{7,8},{8,9},{9,10},{10,1... | collective-permute-start | bytes 995336 | tf_op jit(solution)/shard_map/ppermute | solution.py:22
  413.2 10.9 %collective-permute-start.15 = (f32[3,36,2,384]{3,1,2,0:T(8,128)S(1)}, f32[3,36,2,384]{3,1,2,0:T(8,128)S(1)}, u32[]{:S(2)}, u32[]{:S(2)}) collective-permute-start(f32[3,36,2,384]{3,1,2,0:T(8,128)S(1)} %get-tuple-element.153), channel_id=1, source_target_pairs={{1,0},{2,1},{3,2},{4,3},{5,4},{6,5},{7,6},{8,7},{9,8},{10,9},{11,1... | collective-permute-start | bytes 995336 | tf_op jit(solution)/shard_map/ppermute | solution.py:24
  (21 other events, 175.2 us)
Sparse Core Ops, SparseCore 0:
  62.5 108.3 all-reduce.14
  263.6 111.0 all-reduce.16
where the time goes:
time: 443 us; the launch traced here: 442 us
  waiting for transfers between devices  285 us (64%)
  starting transfers between devices  57.7 us (13%)
  blocking collectives  29.6 us (7%)
  other arithmetic  27.8 us (6%)
  local copies, waits for them, and re-layouts  26.7 us (6%)
  between operations  14.9 us (3%)
    psum x2, waiting for transfers between devices, local(): rows_all = lax.psum(contrib, 'normal')  220 us
    ppermute x8, waiting for transfers between devices, with_halo(): lax.ppermute(head, axis, [((i + 1) % count, i) for i in range(ends)])  44.8 us
    ppermute x8, starting transfers between devices, with_halo(): lax.ppermute(tail, axis, [(i, (i + 1) % count) for i in range(ends)])  37.2 us
    all_gather x2, blocking collectives, local(): lax.all_gather(jnp.stack((minus_own, plus_own, traction_own)), 'normal',...  29.6 us
    unnamed x57, local copies, waits for them, and re-layouts  21.8 us
    ppermute x8, waiting for transfers between devices, with_halo(): lax.ppermute(tail, axis, [(i, (i + 1) % count) for i in range(ends)])  20.9 us
    ppermute x8, starting transfers between devices, with_halo(): lax.ppermute(head, axis, [((i + 1) % count, i) for i in range(ends)])  20.3 us
  transfers between devices with their start and end apart: 18, of which 17 were waited for; matrix products, arithmetic and copies ran while one was open for 1% of the time, Pallas kernels for 0%

commit v1 on v0

--- a/solution.py
+++ b/solution.py
@@ -141,7 +141,7 @@
                 jnp.where(minus_device, traction_row, blank),
             )
         )
-        rows_all = lax.psum(contrib, "normal")
+        rows_all = jnp.sum(lax.all_gather(contrib, "normal"), 0)
         mine = lax.dynamic_slice_in_dim(rows_all, position * owned_rows, owned_rows, 1)
         rate, traction_own, minus_own, plus_own, state_now = friction(
             mine[0], mine[1], mine[2], state_now, mask_now, params

time: 443 us -> 310 us (0.70)
  waiting for transfers between devices: 285 us -> 132 us
  local copies, waits for them, and re-layouts: 26.7 us -> 37 us
    psum x2 -> x0, waiting for transfers between devices: 220 us -> none  [local(): rows_all = lax.psum(contrib, 'normal')]
    all_gather x0 -> x2, waiting for transfers between devices: none -> 71.4 us  [local(): rows_all = jnp.sum(lax.all_gather(contrib, 'normal'), 0)]
    scatter x0 -> x6, local copies, waits for them, and re-layouts: none -> 12 us  [the longest x4 7.71 us: local(): vel_x = vel_x.at[:, last_row, :].set(new_last).at[:, 0, :].set(new_first)]
    ppermute x8, waiting for transfers between devices: 44.8 us -> 39.1 us  [with_halo(): lax.ppermute(head, axis, [((i + 1) % count, i) for i in range(ends)])]
    unnamed x57 -> x64, local copies, waits for them, and re-layouts: 21.8 us -> 16.9 us
  transfers between devices with their start and end apart: 18 -> 18, of which waited for: 17 -> 18; matrix products, arithmetic and copies ran while one was open for 1% -> 3% of each run, Pallas kernels for 0% -> 0%
where the time goes in v1:
time: 310 us; the launch traced here: 309 us
  waiting for transfers between devices  132 us (43%)
  starting transfers between devices  59.5 us (19%)
  local copies, waits for them, and re-layouts  37 us (12%)
  blocking collectives  33 us (11%)
  other arithmetic  31.6 us (10%)
  between operations  14.9 us (5%)
    all_gather x2, waiting for transfers between devices, local(): rows_all = jnp.sum(lax.all_gather(contrib, 'normal'), 0)  71.4 us
    ppermute x8, starting transfers between devices, with_halo(): lax.ppermute(tail, axis, [(i, (i + 1) % count) for i in range(ends)])  39.8 us
    ppermute x8, waiting for transfers between devices, with_halo(): lax.ppermute(head, axis, [((i + 1) % count, i) for i in range(ends)])  39.1 us
    all_gather x2, blocking collectives, local(): lax.all_gather(jnp.stack((minus_own, plus_own, traction_own)), 'normal',...  33 us
    ppermute x8, waiting for transfers between devices, with_halo(): lax.ppermute(tail, axis, [(i, (i + 1) % count) for i in range(ends)])  22 us
    ppermute x8, starting transfers between devices, with_halo(): lax.ppermute(head, axis, [((i + 1) % count, i) for i in range(ends)])  19.6 us
    unnamed x64, local copies, waits for them, and re-layouts  16.9 us
    another operation x6, other arithmetic, accelerate(): return jnp.stack((accel_x, accel_y, accel_z))  8.25 us
  transfers between devices with their start and end apart: 18, of which 18 were waited for; matrix products, arithmetic and copies ran while one was open for 3% of the time, Pallas kernels for 0%

profile of v1, /device:TPU:29, one launch (start us, length us, event | category | flops | bytes accessed | tf_op | source)
XLA Modules:
  0.0 308.7 jit_solution(17931072263525374201)
XLA Ops:
  8.3 3.5 %collective-permute-start.1 = (f32[6,2,16,384]{3,2,1,0:T(8,128)S(1)}, f32[6,2,16,384]{3,2,1,0:T(8,128)S(1)}, u32[]{:S(2)}, u32[]{:S(2)}) collective-permute-start(f32[6,2,16,384]{3,2,1,0:T(8,128)S(1)} %get-tuple-element.142), channel_id=1, source_target_pairs={{0,16},{16,32},{32,48},{48,64},{64,80},{80,96},{96,112},{1,17},{17... | collective-permute-start | bytes 884744 | tf_op jit(solution)/shard_map/ppermute | solution.py:22
  11.8 3.3 %collective-permute-start = (f32[6,2,16,384]{3,2,1,0:T(8,128)S(1)}, f32[6,2,16,384]{3,2,1,0:T(8,128)S(1)}, u32[]{:S(2)}, u32[]{:S(2)}) collective-permute-start(f32[6,2,16,384]{3,2,1,0:T(8,128)S(1)} %get-tuple-element.141), channel_id=1, source_target_pairs={{16,0},{32,16},{48,32},{64,48},{80,64},{96,80},{112,96},{17,1},{33... | collective-permute-start | bytes 884744 | tf_op jit(solution)/shard_map/ppermute | solution.py:24
  15.1 4.5 %collective-permute-done.1 = f32[6,2,16,384]{3,2,1,0:T(8,128)S(1)} collective-permute-done((f32[6,2,16,384]{3,2,1,0:T(8,128)S(1)}, f32[6,2,16,384]{3,2,1,0:T(8,128)S(1)}, u32[]{:S(2)}, u32[]{:S(2)}) %collective-permute-start.1) | collective-permute-done | bytes 294944 | tf_op jit(solution)/shard_map/ppermute | solution.py:22
  19.7 5.1 %constant_dynamic-update-slice_fusion.1 = (f32[6,34,16,384]{3,2,1,0:T(8,128)}, f32[6,36,16,384]{3,2,1,0:T(8,128)S(1)}, f32[6,34,16,384]{3,2,1,0:T(8,128)S(1)}) fusion(f32[6,32,16,384]{3,2,1,0:T(8,128)} %param.25, f32[6,36,16,384]{3,2,1,0:T(8,128)S(1)} %get-tuple-element.170, f32[6,34,16,384]{3,2,1,0:T(8,128)S(1)} %get-tuple-element.169), kind=kLoop, calls=%fused_computation.419 | loop fusion | bytes 18874368
  30.9 3.9 %collective-permute-start.2 = (f32[6,36,2,384]{3,2,1,0:T(2,128)S(1)}, f32[6,36,2,384]{3,2,1,0:T(2,128)S(1)}, u32[]{:S(2)}, u32[]{:S(2)}) collective-permute-start(f32[6,36,2,384]{3,2,1,0:T(2,128)S(1)} %get-tuple-element.126), channel_id=1, source_target_pairs={{0,1},{1,2},{2,3},{3,4},{4,5},{5,6},{6,7},{7,8},{8,9},{9,10},{10,1... | collective-permute-start | bytes 1990664 | tf_op jit(solution)/shard_map/ppermute | solution.py:22
  42.4 6.5 %collective-permute-done.3 = f32[6,36,2,384]{3,2,1,0:T(2,128)S(1)} collective-permute-done((f32[6,36,2,384]{3,2,1,0:T(2,128)S(1)}, f32[6,36,2,384]{3,2,1,0:T(2,128)S(1)}, u32[]{:S(2)}, u32[]{:S(2)}) %collective-permute-start.3) | collective-permute-done | bytes 663584 | tf_op jit(solution)/shard_map/ppermute | solution.py:24
  58.2 34.8 %all-gather.5.cloned.1.call-done = f32[48,32,384]{2,1,0:T(8,128)} async-done(((f32[3,32,384]{2,1,0:T(8,128)}), f32[48,32,384]{2,1,0:T(8,128)}) %all-gather.5.cloned.1.call-update) | async-done | bytes 2359312 | tf_op jit(solution)/shard_map/all_gather | solution.py:144
  95.0 16.5 %all_gather.20 = f32[3,32,384]{2,0,1:T(4,128)S(1)} all-gather(f32[3,2,384]{2,0,1:T(4,128)S(1)} %copy.34), channel_id=1, replica_groups=mesh['strike'=8,'normal'=16] {'normal'}, dimensions={1}, use_global_device_ids=true | all-gather | bytes 156672 | tf_op jit(solution)/shard_map/all_gather | solution.py:149
  117.7 3.8 %collective-permute-start.4 = (f32[3,2,16,384]{3,2,1,0:T(8,128)S(1)}, f32[3,2,16,384]{3,2,1,0:T(8,128)S(1)}, u32[]{:S(2)}, u32[]{:S(2)}) collective-permute-start(f32[3,2,16,384]{3,2,1,0:T(8,128)S(1)} %get-tuple-element.159), channel_id=1, source_target_pairs={{0,16},{16,32},{32,48},{48,64},{64,80},{80,96},{96,112},{1,17},{17... | collective-permute-start | bytes 442376 | tf_op jit(solution)/shard_map/ppermute | solution.py:22
  121.4 3.2 %collective-permute-start.5 = (f32[3,2,16,384]{3,2,1,0:T(8,128)S(1)}, f32[3,2,16,384]{3,2,1,0:T(8,128)S(1)}, u32[]{:S(2)}, u32[]{:S(2)}) collective-permute-start(f32[3,2,16,384]{3,2,1,0:T(8,128)S(1)} %get-tuple-element.160), channel_id=1, source_target_pairs={{16,0},{32,16},{48,32},{64,48},{80,64},{96,80},{112,96},{17,1},{33... | collective-permute-start | bytes 442376 | tf_op jit(solution)/shard_map/ppermute | solution.py:24
  126.5 4.2 %collective-permute-done.5 = f32[3,2,16,384]{3,2,1,0:T(8,128)S(1)} collective-permute-done((f32[3,2,16,384]{3,2,1,0:T(8,128)S(1)}, f32[3,2,16,384]{3,2,1,0:T(8,128)S(1)}, u32[]{:S(2)}, u32[]{:S(2)}) %collective-permute-start.5) | collective-permute-done | bytes 147488 | tf_op jit(solution)/shard_map/ppermute | solution.py:24
  130.9 7.5 %collective-permute-start.6 = (f32[3,36,2,384]{3,2,1,0:T(2,128)S(1)}, f32[3,36,2,384]{3,2,1,0:T(2,128)S(1)}, u32[]{:S(2)}, u32[]{:S(2)}) collective-permute-start(f32[3,36,2,384]{3,2,1,0:T(2,128)S(1)} %get-tuple-element.151), channel_id=1, source_target_pairs={{0,1},{1,2},{2,3},{3,4},{4,5},{5,6},{6,7},{7,8},{8,9},{9,10},{10,1... | collective-permute-start | bytes 995336 | tf_op jit(solution)/shard_map/ppermute | solution.py:22
  142.4 6.5 %collective-permute-done.7 = f32[3,36,2,384]{3,2,1,0:T(2,128)S(1)} collective-permute-done((f32[3,36,2,384]{3,2,1,0:T(2,128)S(1)}, f32[3,36,2,384]{3,2,1,0:T(2,128)S(1)}, u32[]{:S(2)}, u32[]{:S(2)}) %collective-permute-start.7) | collective-permute-done | bytes 331808 | tf_op jit(solution)/shard_map/ppermute | solution.py:24
  161.3 6.0 %collective-permute-start.9 = (f32[6,2,16,384]{3,2,1,0:T(8,128)S(1)}, f32[6,2,16,384]{3,2,1,0:T(8,128)S(1)}, u32[]{:S(2)}, u32[]{:S(2)}) collective-permute-start(f32[6,2,16,384]{3,2,1,0:T(8,128)S(1)} %get-tuple-element.132), channel_id=1, source_target_pairs={{0,16},{16,32},{32,48},{48,64},{64,80},{80,96},{96,112},{1,17},{17... | collective-permute-start | bytes 884744 | tf_op jit(solution)/shard_map/ppermute | solution.py:22
  174.1 4.1 %collective-permute-start.10 = (f32[6,36,2,384]{3,2,1,0:T(2,128)S(1)}, f32[6,36,2,384]{3,2,1,0:T(2,128)S(1)}, u32[]{:S(2)}, u32[]{:S(2)}) collective-permute-start(f32[6,36,2,384]{3,2,1,0:T(2,128)S(1)} %get-tuple-element.124), channel_id=1, source_target_pairs={{0,1},{1,2},{2,3},{3,4},{4,5},{5,6},{6,7},{7,8},{8,9},{9,10},{10,1... | collective-permute-start | bytes 1990664 | tf_op jit(solution)/shard_map/ppermute | solution.py:22
  180.5 5.3 %collective-permute-done.10 = f32[6,36,2,384]{3,2,1,0:T(2,128)S(1)} collective-permute-done((f32[6,36,2,384]{3,2,1,0:T(2,128)S(1)}, f32[6,36,2,384]{3,2,1,0:T(2,128)S(1)}, u32[]{:S(2)}, u32[]{:S(2)}) %collective-permute-start.10) | collective-permute-done | bytes 663584 | tf_op jit(solution)/shard_map/ppermute | solution.py:22
  185.8 6.5 %collective-permute-done.11 = f32[6,36,2,384]{3,2,1,0:T(2,128)S(1)} collective-permute-done((f32[6,36,2,384]{3,2,1,0:T(2,128)S(1)}, f32[6,36,2,384]{3,2,1,0:T(2,128)S(1)}, u32[]{:S(2)}, u32[]{:S(2)}) %collective-permute-start.11) | collective-permute-done | bytes 663584 | tf_op jit(solution)/shard_map/ppermute | solution.py:24
  199.1 36.7 %all-gather.7.cloned.1.call-done = f32[48,32,384]{2,1,0:T(8,128)} async-done(((f32[3,32,384]{2,1,0:T(8,128)}), f32[48,32,384]{2,1,0:T(8,128)}) %all-gather.7.cloned.1.call-update) | async-done | bytes 2359312 | tf_op jit(solution)/shard_map/all_gather | solution.py:144
  238.4 16.5 %all_gather.23 = f32[3,32,384]{2,0,1:T(4,128)S(1)} all-gather(f32[3,2,384]{2,0,1:T(4,128)S(1)} %copy.37), channel_id=1, replica_groups=mesh['strike'=8,'normal'=16] {'normal'}, dimensions={1}, use_global_device_ids=true | all-gather | bytes 156672 | tf_op jit(solution)/shard_map/all_gather | solution.py:149
  261.0 3.6 %collective-permute-start.12 = (f32[3,2,16,384]{3,2,1,0:T(8,128)S(1)}, f32[3,2,16,384]{3,2,1,0:T(8,128)S(1)}, u32[]{:S(2)}, u32[]{:S(2)}) collective-permute-start(f32[3,2,16,384]{3,2,1,0:T(8,128)S(1)} %get-tuple-element.154), channel_id=1, source_target_pairs={{0,16},{16,32},{32,48},{48,64},{64,80},{80,96},{96,112},{1,17},{17... | collective-permute-start | bytes 442376 | tf_op jit(solution)/shard_map/ppermute | solution.py:22
  264.6 3.2 %collective-permute-start.13 = (f32[3,2,16,384]{3,2,1,0:T(8,128)S(1)}, f32[3,2,16,384]{3,2,1,0:T(8,128)S(1)}, u32[]{:S(2)}, u32[]{:S(2)}) collective-permute-start(f32[3,2,16,384]{3,2,1,0:T(8,128)S(1)} %get-tuple-element.155), channel_id=1, source_target_pairs={{16,0},{32,16},{48,32},{64,48},{80,64},{96,80},{112,96},{17,1},{33... | collective-permute-start | bytes 442376 | tf_op jit(solution)/shard_map/ppermute | solution.py:24
  269.7 4.2 %collective-permute-done.13 = f32[3,2,16,384]{3,2,1,0:T(8,128)S(1)} collective-permute-done((f32[3,2,16,384]{3,2,1,0:T(8,128)S(1)}, f32[3,2,16,384]{3,2,1,0:T(8,128)S(1)}, u32[]{:S(2)}, u32[]{:S(2)}) %collective-permute-start.13) | collective-permute-done | bytes 147488 | tf_op jit(solution)/shard_map/ppermute | solution.py:24
  274.1 7.5 %collective-permute-start.14 = (f32[3,36,2,384]{3,2,1,0:T(2,128)S(1)}, f32[3,36,2,384]{3,2,1,0:T(2,128)S(1)}, u32[]{:S(2)}, u32[]{:S(2)}) collective-permute-start(f32[3,36,2,384]{3,2,1,0:T(2,128)S(1)} %get-tuple-element.149), channel_id=1, source_target_pairs={{0,1},{1,2},{2,3},{3,4},{4,5},{5,6},{6,7},{7,8},{8,9},{9,10},{10,1... | collective-permute-start | bytes 995336 | tf_op jit(solution)/shard_map/ppermute | solution.py:22
  285.6 6.5 %collective-permute-done.15 = f32[3,36,2,384]{3,2,1,0:T(2,128)S(1)} collective-permute-done((f32[3,36,2,384]{3,2,1,0:T(2,128)S(1)}, f32[3,36,2,384]{3,2,1,0:T(2,128)S(1)}, u32[]{:S(2)}, u32[]{:S(2)}) %collective-permute-start.15) | collective-permute-done | bytes 331808 | tf_op jit(solution)/shard_map/ppermute | solution.py:24
  (162 shorter events, 90.5 us)
Async XLA Ops:
  7.2 50.9 %copy-start = (f32[4,4]{1,0:T(4,128)S(1)}, f32[4,4]{1,0:T(4,128)}, u32[]{:S(2)}) copy-start(f32[4,4]{1,0:T(4,128)} %param.31) | copy-start | bytes 196
  7.2 85.8 %all-gather.5.cloned.1.call-start = ((), (), s32[]{:S(2)}) async-start(), calls=%async_computation | async-start | bytes 2506752 | tf_op jit(solution)/shard_map/all_gather | solution.py:144
  8.3 11.3 %collective-permute-start.1 = (f32[6,2,16,384]{3,2,1,0:T(8,128)S(1)}, f32[6,2,16,384]{3,2,1,0:T(8,128)S(1)}, u32[]{:S(2)}, u32[]{:S(2)}) collective-permute-start(f32[6,2,16,384]{3,2,1,0:T(8,128)S(1)} %get-tuple-element.142), channel_id=1, source_target_pairs={{0,16},{16,32},{32,48},{48,64},{64,80},{80,96},{96,112},{1,17},{17... | collective-permute-start | bytes 884744 | tf_op jit(solution)/shard_map/ppermute | solution.py:22
  11.8 15.5 %collective-permute-start = (f32[6,2,16,384]{3,2,1,0:T(8,128)S(1)}, f32[6,2,16,384]{3,2,1,0:T(8,128)S(1)}, u32[]{:S(2)}, u32[]{:S(2)}) collective-permute-start(f32[6,2,16,384]{3,2,1,0:T(8,128)S(1)} %get-tuple-element.141), channel_id=1, source_target_pairs={{16,0},{32,16},{48,32},{64,48},{80,64},{96,80},{112,96},{17,1},{33... | collective-permute-start | bytes 884744 | tf_op jit(solution)/shard_map/ppermute | solution.py:24
  30.9 11.5 %collective-permute-start.2 = (f32[6,36,2,384]{3,2,1,0:T(2,128)S(1)}, f32[6,36,2,384]{3,2,1,0:T(2,128)S(1)}, u32[]{:S(2)}, u32[]{:S(2)}) collective-permute-start(f32[6,36,2,384]{3,2,1,0:T(2,128)S(1)} %get-tuple-element.126), channel_id=1, source_target_pairs={{0,1},{1,2},{2,3},{3,4},{4,5},{5,6},{6,7},{7,8},{8,9},{9,10},{10,1... | collective-permute-start | bytes 1990664 | tf_op jit(solution)/shard_map/ppermute | solution.py:22
  34.8 14.1 %collective-permute-start.3 = (f32[6,36,2,384]{3,2,1,0:T(2,128)S(1)}, f32[6,36,2,384]{3,2,1,0:T(2,128)S(1)}, u32[]{:S(2)}, u32[]{:S(2)}) collective-permute-start(f32[6,36,2,384]{3,2,1,0:T(2,128)S(1)} %get-tuple-element.127), channel_id=1, source_target_pairs={{1,0},{2,1},{3,2},{4,3},{5,4},{6,5},{7,6},{8,7},{9,8},{10,9},{11,1... | collective-permute-start | bytes 1990664 | tf_op jit(solution)/shard_map/ppermute | solution.py:24
  56.1 38.7 %copy-start.21 = (s32[2,384]{1,0:T(2,128)S(1)}, s32[2,384]{1,0:T(2,128)}, u32[]{:S(2)}) copy-start(s32[2,384]{1,0:T(2,128)} %param.29) | copy-start | bytes 9220
  56.1 38.7 %copy-start.23 = (f32[2,384]{1,0:T(2,128)S(1)}, f32[2,384]{1,0:T(2,128)}, u32[]{:S(2)}) copy-start(f32[2,384]{1,0:T(2,128)} %param.28) | copy-start | bytes 9220
  58.0 177.8 %all-gather.7.cloned.1.call-start = ((), (), s32[]{:S(2)}) async-start(), calls=%async_computation.1 | async-start | bytes 2506752 | tf_op jit(solution)/shard_map/all_gather | solution.py:144
  117.7 8.8 %collective-permute-start.4 = (f32[3,2,16,384]{3,2,1,0:T(8,128)S(1)}, f32[3,2,16,384]{3,2,1,0:T(8,128)S(1)}, u32[]{:S(2)}, u32[]{:S(2)}) collective-permute-start(f32[3,2,16,384]{3,2,1,0:T(8,128)S(1)} %get-tuple-element.159), channel_id=1, source_target_pairs={{0,16},{16,32},{32,48},{48,64},{64,80},{80,96},{96,112},{1,17},{17... | collective-permute-start | bytes 442376 | tf_op jit(solution)/shard_map/ppermute | solution.py:22
  121.4 9.3 %collective-permute-start.5 = (f32[3,2,16,384]{3,2,1,0:T(8,128)S(1)}, f32[3,2,16,384]{3,2,1,0:T(8,128)S(1)}, u32[]{:S(2)}, u32[]{:S(2)}) collective-permute-start(f32[3,2,16,384]{3,2,1,0:T(8,128)S(1)} %get-tuple-element.160), channel_id=1, source_target_pairs={{16,0},{32,16},{48,32},{64,48},{80,64},{96,80},{112,96},{17,1},{33... | collective-permute-start | bytes 442376 | tf_op jit(solution)/shard_map/ppermute | solution.py:24
  130.9 11.5 %collective-permute-start.6 = (f32[3,36,2,384]{3,2,1,0:T(2,128)S(1)}, f32[3,36,2,384]{3,2,1,0:T(2,128)S(1)}, u32[]{:S(2)}, u32[]{:S(2)}) collective-permute-start(f32[3,36,2,384]{3,2,1,0:T(2,128)S(1)} %get-tuple-element.151), channel_id=1, source_target_pairs={{0,1},{1,2},{2,3},{3,4},{4,5},{5,6},{6,7},{7,8},{8,9},{9,10},{10,1... | collective-permute-start | bytes 995336 | tf_op jit(solution)/shard_map/ppermute | solution.py:22
  138.4 10.5 %collective-permute-start.7 = (f32[3,36,2,384]{3,2,1,0:T(2,128)S(1)}, f32[3,36,2,384]{3,2,1,0:T(2,128)S(1)}, u32[]{:S(2)}, u32[]{:S(2)}) collective-permute-start(f32[3,36,2,384]{3,2,1,0:T(2,128)S(1)} %get-tuple-element.152), channel_id=1, source_target_pairs={{1,0},{2,1},{3,2},{4,3},{5,4},{6,5},{7,6},{8,7},{9,8},{10,9},{11,1... | collective-permute-start | bytes 995336 | tf_op jit(solution)/shard_map/ppermute | solution.py:24
  159.3 10.1 %collective-permute-start.8 = (f32[6,2,16,384]{3,2,1,0:T(8,128)S(1)}, f32[6,2,16,384]{3,2,1,0:T(8,128)S(1)}, u32[]{:S(2)}, u32[]{:S(2)}) collective-permute-start(f32[6,2,16,384]{3,2,1,0:T(8,128)S(1)} %get-tuple-element.133), channel_id=1, source_target_pairs={{16,0},{32,16},{48,32},{64,48},{80,64},{96,80},{112,96},{17,1},{33... | collective-permute-start | bytes 884744 | tf_op jit(solution)/shard_map/ppermute | solution.py:24
  161.3 10.0 %collective-permute-start.9 = (f32[6,2,16,384]{3,2,1,0:T(8,128)S(1)}, f32[6,2,16,384]{3,2,1,0:T(8,128)S(1)}, u32[]{:S(2)}, u32[]{:S(2)}) collective-permute-start(f32[6,2,16,384]{3,2,1,0:T(8,128)S(1)} %get-tuple-element.132), channel_id=1, source_target_pairs={{0,16},{16,32},{32,48},{48,64},{64,80},{80,96},{96,112},{1,17},{17... | collective-permute-start | bytes 884744 | tf_op jit(solution)/shard_map/ppermute | solution.py:22
  174.1 11.7 %collective-permute-start.10 = (f32[6,36,2,384]{3,2,1,0:T(2,128)S(1)}, f32[6,36,2,384]{3,2,1,0:T(2,128)S(1)}, u32[]{:S(2)}, u32[]{:S(2)}) collective-permute-start(f32[6,36,2,384]{3,2,1,0:T(2,128)S(1)} %get-tuple-element.124), channel_id=1, source_target_pairs={{0,1},{1,2},{2,3},{3,4},{4,5},{5,6},{6,7},{7,8},{8,9},{9,10},{10,1... | collective-permute-start | bytes 1990664 | tf_op jit(solution)/shard_map/ppermute | solution.py:22
  178.2 14.1 %collective-permute-start.11 = (f32[6,36,2,384]{3,2,1,0:T(2,128)S(1)}, f32[6,36,2,384]{3,2,1,0:T(2,128)S(1)}, u32[]{:S(2)}, u32[]{:S(2)}) collective-permute-start(f32[6,36,2,384]{3,2,1,0:T(2,128)S(1)} %get-tuple-element.125), channel_id=1, source_target_pairs={{1,0},{2,1},{3,2},{4,3},{5,4},{6,5},{7,6},{8,7},{9,8},{10,9},{11,1... | collective-permute-start | bytes 1990664 | tf_op jit(solution)/shard_map/ppermute | solution.py:24
  197.3 63.6 %copy-start.5 = (f32[3,32,16,384]{3,2,1,0:T(8,128)S(1)}, f32[3,32,16,384]{3,2,1,0:T(8,128)}, u32[]{:S(2)}) copy-start(f32[3,32,16,384]{3,2,1,0:T(8,128)} %copy-done.4) | copy-start | bytes 7077892
  238.3 35.8 %copy-start.22 = (f32[2,384]{1,0:T(2,128)}, f32[2,384]{1,0:T(2,128)S(1)}, u32[]{:S(2)}) copy-start(f32[2,384]{1,0:T(2,128)S(1)} %get-tuple-element.105) | copy-start | bytes 9220
  260.9 33.4 %copy-start.6 = (f32[3,32,16,384]{3,2,1,0:T(8,128)}, f32[3,32,16,384]{3,2,1,0:T(8,128)S(1)}, u32[]{:S(2)}) copy-start(f32[3,32,16,384]{3,2,1,0:T(8,128)S(1)} %constant_dynamic-update-slice_fusion.7) | copy-start | bytes 7077892
  261.0 8.7 %collective-permute-start.12 = (f32[3,2,16,384]{3,2,1,0:T(8,128)S(1)}, f32[3,2,16,384]{3,2,1,0:T(8,128)S(1)}, u32[]{:S(2)}, u32[]{:S(2)}) collective-permute-start(f32[3,2,16,384]{3,2,1,0:T(8,128)S(1)} %get-tuple-element.154), channel_id=1, source_target_pairs={{0,16},{16,32},{32,48},{48,64},{64,80},{80,96},{96,112},{1,17},{17... | collective-permute-start | bytes 442376 | tf_op jit(solution)/shard_map/ppermute | solution.py:22
  264.6 9.3 %collective-permute-start.13 = (f32[3,2,16,384]{3,2,1,0:T(8,128)S(1)}, f32[3,2,16,384]{3,2,1,0:T(8,128)S(1)}, u32[]{:S(2)}, u32[]{:S(2)}) collective-permute-start(f32[3,2,16,384]{3,2,1,0:T(8,128)S(1)} %get-tuple-element.155), channel_id=1, source_target_pairs={{16,0},{32,16},{48,32},{64,48},{80,64},{96,80},{112,96},{17,1},{33... | collective-permute-start | bytes 442376 | tf_op jit(solution)/shard_map/ppermute | solution.py:24
  274.1 11.5 %collective-permute-start.14 = (f32[3,36,2,384]{3,2,1,0:T(2,128)S(1)}, f32[3,36,2,384]{3,2,1,0:T(2,128)S(1)}, u32[]{:S(2)}, u32[]{:S(2)}) collective-permute-start(f32[3,36,2,384]{3,2,1,0:T(2,128)S(1)} %get-tuple-element.149), channel_id=1, source_target_pairs={{0,1},{1,2},{2,3},{3,4},{4,5},{5,6},{6,7},{7,8},{8,9},{9,10},{10,1... | collective-permute-start | bytes 995336 | tf_op jit(solution)/shard_map/ppermute | solution.py:22
  281.6 10.5 %collective-permute-start.15 = (f32[3,36,2,384]{3,2,1,0:T(2,128)S(1)}, f32[3,36,2,384]{3,2,1,0:T(2,128)S(1)}, u32[]{:S(2)}, u32[]{:S(2)}) collective-permute-start(f32[3,36,2,384]{3,2,1,0:T(2,128)S(1)} %get-tuple-element.150), channel_id=1, source_target_pairs={{1,0},{2,1},{3,2},{4,3},{5,4},{6,5},{7,6},{8,7},{9,8},{10,9},{11,1... | collective-permute-start | bytes 995336 | tf_op jit(solution)/shard_map/ppermute | solution.py:24
  (25 other events, 165.7 us)
Sparse Core Ops, SparseCore 0:
  58.1 34.8 all-gather.4
  199.2 36.4 all-gather.6
